TPU v7x, 32 devices: a whole 2x2x4 slice. The times are simulated.
32 devices in a mesh: dp: 8 (over y, x, core), mp: 4 (over z).
Axes of the slice: x: 2, y: 2, z: 4, core: 2. Of those that a mesh axis runs over, the one named last changes fastest.
Arguments:
- inputs: bfloat16 [8192, 2048], P('dp'), may hold values from -8 to 8
- segment_ids: int32 [8, 1024], P('dp'), may hold values from 0 to 4, as said below
- pad_count: int32 [8], P('dp'), may hold values from 0 to 128, as said below
- layer_norm_gain: float32 [2048], replicated, may hold values from 0.5 to 1.5
- layer_norm_bias: float32 [2048], replicated, may hold values from -1.75 to 1.75
- qkv_weight: bfloat16 [2048, 3, 2048], P(None, None, 'mp'), may hold values from -0.125 to 0.125
- qkv_bias: float32 [3, 2048], P(None, 'mp'), may hold values from -1.75 to 1.75
- out_weight: bfloat16 [2048, 2048], P('mp'), may hold values from -1 to 1
- gateup_weight: bfloat16 [2048, 2, 5632], P(None, None, 'mp'), may hold values from -0.125 to 0.125
- down_weight: bfloat16 [5632, 2048], P('mp'), may hold values from -0.078125 to 0.078125
- y_grad: bfloat16 [8192, 2048], P('dp'), may hold values from -8 to 8
Outputs:
- output: bfloat16 [8192, 2048], P('dp')
- x_grad: bfloat16 [8192, 2048], P('dp')
- ln_gain_grad: float32 [2048], replicated
- ln_bias_grad: float32 [2048], replicated
- qkv_weight_grad: float32 [2048, 3, 2048], P('dp', None, 'mp')
- qkv_bias_grad: float32 [3, 2048], P(None, 'mp')
- out_weight_grad: float32 [2048, 2048], P('mp', 'dp')
- gateup_weight_grad: float32 [2048, 2, 5632], P('dp', None, 'mp')
- down_weight_grad: float32 [5632, 2048], P('mp', 'dp')
Inputs may be any that keep to these rules, and one draw needn't show every extreme that they name: `segment_ids`: within a row the ids never fall and run from 0 to 4 - 1 over the row's documents, each of 1 or more tokens and one of exactly 512; the row's last pad_count slots carry id 4. `pad_count`: some row has 128 padded slots and some row has none.
All inputs are finite; a program needn't handle non-finite values.
Results may differ from a plain program's by a relative error of at most 0.012.
The roundings to bfloat16 on the way count: a program that leaves them out, or rounds other values in their place, can miss the bound.
Values may be sent and summed in bfloat16 or wider, within the bound.
No kernel may reach another device: no remote copies, remote signals or barrier semaphores. Data moves between devices by JAX's collectives and lax.ppermute only.
A program may use at most 256 MiB of HBM per device.

v0:
```python
import jax
import jax.numpy as jnp
from jax import lax
from jax.sharding import PartitionSpec as P

HEAD_DIM = 64
ROT = 16
DOCS = 4
EPS = 1e-05


def tables(seg, padding, count):
    steps = jnp.arange(count, dtype=jnp.int32)
    onehot = (seg[:, None] == jnp.arange(DOCS + 1, dtype=jnp.int32)[None, :]).astype(jnp.int32)
    counts = jnp.sum(onehot, axis=0)
    before = jnp.cumsum(counts) - counts
    start = jnp.sum(onehot * before[None, :], axis=1)
    half = ROT // 2
    freq = jnp.power(10000.0, -2.0 * jnp.arange(half, dtype=jnp.float32) / ROT)
    angle = (steps - start).astype(jnp.float32)[:, None] * freq[None, :]
    return (jnp.cos(angle)[:, None, :], jnp.sin(angle)[:, None, :], steps < count - padding)


def rotate(value, cosine, sine):
    half = ROT // 2
    first = value[..., :half]
    second = value[..., half:ROT]
    return jnp.concatenate(
        [first * cosine - second * sine, second * cosine + first * sine, value[..., ROT:]], axis=-1
    )


def unrotate(value, cosine, sine):
    half = ROT // 2
    first = value[..., :half]
    second = value[..., half:ROT]
    return jnp.concatenate(
        [first * cosine + second * sine, second * cosine - first * sine, value[..., ROT:]], axis=-1
    )


def allowed_mask(start, block_rows, seg, valid):
    count = seg.shape[0]
    rows = start + jnp.arange(block_rows, dtype=jnp.int32)
    cols = jnp.arange(count, dtype=jnp.int32)
    seg_rows = lax.dynamic_slice_in_dim(seg, start, block_rows, 0)
    allowed = (
        (seg_rows[:, None] == seg[None, :]) & (cols[None, :] <= rows[:, None]) & valid[None, :]
    )
    return allowed | (cols[None, :] == rows[:, None])


def scores(start, block_rows, query, key, seg, valid):
    part = lax.dynamic_slice_in_dim(query, start, block_rows, 0)
    score = jnp.einsum(
        "qhd,khd->hqk", part, key, preferred_element_type=jnp.float32
    ) * HEAD_DIM ** (-0.5)
    allowed = allowed_mask(start, block_rows, seg, valid)
    return (part, jnp.where(allowed[None], score, -1e30), allowed)


def shards(
    inputs,
    segment_ids,
    pad_count,
    layer_norm_gain,
    layer_norm_bias,
    qkv_weight,
    qkv_bias,
    out_weight,
    gateup_weight,
    down_weight,
    y_grad,
):
    count, width = inputs.shape
    local = qkv_weight.shape[2]
    hidden_here = gateup_weight.shape[2]
    heads_here = local // HEAD_DIM
    seg = segment_ids[0]
    cosine, sine, valid = tables(seg, pad_count[0], count)
    valid_f = valid.astype(jnp.float32)
    xf = inputs.astype(jnp.float32)
    row_average = jnp.mean(xf, axis=-1, keepdims=True)
    mean_removed = xf - row_average
    var = jnp.mean(mean_removed * mean_removed, axis=-1, keepdims=True)
    inverse_deviation = lax.rsqrt(var + EPS)
    standardized_input = mean_removed * inverse_deviation
    norm_output = (standardized_input * layer_norm_gain + layer_norm_bias).astype(jnp.bfloat16)
    qkv = jnp.dot(
        norm_output, qkv_weight.reshape(width, 3 * local), preferred_element_type=jnp.float32
    )
    qkv = qkv.reshape(count, 3, local) + qkv_bias
    query = rotate(qkv[:, 0].reshape(count, heads_here, HEAD_DIM), cosine, sine).astype(
        jnp.bfloat16
    )
    key = rotate(qkv[:, 1].reshape(count, heads_here, HEAD_DIM), cosine, sine).astype(jnp.bfloat16)
    value = qkv[:, 2].reshape(count, heads_here, HEAD_DIM).astype(jnp.bfloat16)
    block_rows = min(512, count)
    starts = jnp.arange(count // block_rows, dtype=jnp.int32) * block_rows

    def forward_block(start):
        part, score, allowed = scores(start, block_rows, query, key, seg, valid)
        top = jnp.max(score, axis=-1, keepdims=True)
        expo = jnp.exp(score - top)
        total = jnp.sum(expo, axis=-1, keepdims=True)
        prob = (expo / total).astype(jnp.bfloat16)
        return (
            jnp.einsum("hqk,khd->qhd", prob, value, preferred_element_type=jnp.float32),
            (top + jnp.log(total))[..., 0],
        )

    attn_blocks, log_sums = lax.map(forward_block, starts)
    attn = (attn_blocks.reshape(count, local) * valid_f[:, None]).astype(jnp.bfloat16)
    gateup = jnp.dot(
        norm_output,
        gateup_weight.reshape(width, 2 * hidden_here),
        preferred_element_type=jnp.float32,
    )
    gateup = gateup.reshape(count, 2, hidden_here)
    gate = gateup[:, 0]
    upper = gateup[:, 1]
    sigma = jax.nn.sigmoid(gate)
    active = gate * sigma
    hidden = (active * upper).astype(jnp.bfloat16)
    partial_value = jnp.dot(attn, out_weight, preferred_element_type=jnp.float32) + jnp.dot(
        hidden, down_weight, preferred_element_type=jnp.float32
    )
    summed = lax.psum(partial_value, "mp")
    result = (xf + summed).astype(jnp.bfloat16)
    grad_out = jnp.einsum("ti,to->io", attn, y_grad, preferred_element_type=jnp.float32)
    grad_down = jnp.einsum("tf,to->fo", hidden, y_grad, preferred_element_type=jnp.float32)
    d_attn = jnp.einsum("to,io->ti", y_grad, out_weight, preferred_element_type=jnp.float32)
    d_attn = (d_attn.astype(jnp.bfloat16) * valid.astype(jnp.bfloat16)[:, None]).reshape(
        count, heads_here, HEAD_DIM
    )
    d_hidden = jnp.einsum("to,fo->tf", y_grad, down_weight, preferred_element_type=jnp.float32)
    d_gate = (d_hidden * upper * sigma * (1.0 + gate * (1.0 - sigma))).astype(jnp.bfloat16)
    d_upper = (d_hidden * active).astype(jnp.bfloat16)
    d_gateup = jnp.stack([d_gate, d_upper], axis=1)
    grad_gateup = jnp.einsum(
        "td,tjf->djf", norm_output, d_gateup, preferred_element_type=jnp.float32
    )

    def backward_block(carry, item):
        key_acc, value_acc = carry
        start, log_sum = item
        part, score, allowed = scores(start, block_rows, query, key, seg, valid)
        prob = jnp.where(allowed[None], jnp.exp(score - log_sum[..., None]), 0.0)
        prob_low = prob.astype(jnp.bfloat16)
        d_rows = lax.dynamic_slice_in_dim(d_attn, start, block_rows, 0)
        d_prob = jnp.einsum("qhd,khd->hqk", d_rows, value, preferred_element_type=jnp.float32)
        d_score = prob * (d_prob - jnp.sum(prob * d_prob, axis=-1, keepdims=True))
        d_score = d_score.astype(jnp.bfloat16)
        d_query = jnp.einsum(
            "hqk,khd->qhd", d_score, key, preferred_element_type=jnp.float32
        ) * HEAD_DIM ** (-0.5)
        key_acc = key_acc + jnp.einsum(
            "hqk,qhd->khd", d_score, part, preferred_element_type=jnp.float32
        ) * HEAD_DIM ** (-0.5)
        value_acc = value_acc + jnp.einsum(
            "hqk,qhd->khd", prob_low, d_rows, preferred_element_type=jnp.float32
        )
        return ((key_acc, value_acc), d_query)

    empty = jnp.zeros((count, heads_here, HEAD_DIM), jnp.float32)
    (d_key, d_value), d_queries = lax.scan(backward_block, (empty, empty), (starts, log_sums))
    d_query = unrotate(d_queries.reshape(count, heads_here, HEAD_DIM), cosine, sine)
    d_key = unrotate(d_key, cosine, sine)
    d_qkv = (
        jnp.stack([d_query, d_key, d_value], axis=1).reshape(count, 3, local).astype(jnp.bfloat16)
    )
    grad_qkv = jnp.einsum("td,tjc->djc", norm_output, d_qkv, preferred_element_type=jnp.float32)
    grad_bias = jnp.sum(d_qkv.astype(jnp.float32), axis=0)
    weight_sums = (
        lax.psum_scatter(grad_qkv, "dp", scatter_dimension=0, tiled=True),
        lax.psum_scatter(grad_out, "dp", scatter_dimension=1, tiled=True),
        lax.psum_scatter(grad_gateup, "dp", scatter_dimension=0, tiled=True),
        lax.psum_scatter(grad_down, "dp", scatter_dimension=1, tiled=True),
    )
    d_partial = jnp.einsum(
        "tjc,djc->td", d_qkv, qkv_weight, preferred_element_type=jnp.float32
    ) + jnp.einsum("tjf,djf->td", d_gateup, gateup_weight, preferred_element_type=jnp.float32)
    normalized_gradient = lax.psum(d_partial, "mp")
    gain_product = jnp.sum(normalized_gradient * standardized_input, axis=0)
    shift_part = jnp.sum(normalized_gradient, axis=0)
    gain_scaled = normalized_gradient * layer_norm_gain
    inner = (
        gain_scaled
        - jnp.mean(gain_scaled, axis=-1, keepdims=True)
        - standardized_input * jnp.mean(gain_scaled * standardized_input, axis=-1, keepdims=True)
    )
    input_grad = (y_grad.astype(jnp.float32) + inverse_deviation * inner).astype(jnp.bfloat16)
    bias_sum, gain_sum, shift_sum = lax.psum((grad_bias, gain_product, shift_part), "dp")
    return (
        result,
        input_grad,
        gain_sum,
        shift_sum,
        weight_sums[0],
        bias_sum,
        weight_sums[1],
        weight_sums[2],
        weight_sums[3],
    )


def solution(mesh):
    placed = (
        P("dp", None),
        P("dp", None),
        P("dp"),
        P(),
        P(),
        P(None, None, "mp"),
        P(None, "mp"),
        P("mp", None),
        P(None, None, "mp"),
        P("mp", None),
        P("dp", None),
    )
    return jax.shard_map(
        shards,
        mesh=mesh,
        in_specs=placed,
        out_specs=(
            P("dp", None),
            P("dp", None),
            P(),
            P(),
            P("dp", None, "mp"),
            P(None, "mp"),
            P("mp", "dp"),
            P("dp", None, "mp"),
            P("mp", "dp"),
        ),
        check_vma=False,
    )
```

profile of v0, /device:TPU:0, one launch (start us, length us, event | category | flops | bytes accessed | tf_op | source)
XLA Modules:
  0.0 1045.4 jit_solution(3423792791581384292)
XLA Ops:
  12.9 8.9 copy.39
  21.8 10.5 %broadcast_add_fusion = f32[1024,3,512]{0,2,1:T(8,128)S(1)} fusion(f32[3,512]{1,0:T(4,128)S(1)} %copy-done.24, bf16[2048,3,512]{0,2,1:T(8,128)(2,1)} %copy.39, bf16[1024,2048]{1,0:T(8,128)(2,1)} %param.15, f32[2048]{0:T(1024)S(1)} %copy-done.25, f32[2048]{0:T(1024)S(1)} %copy-done.21, f32[1024]{0:T(1024)S(1)} %add_rsqrt_fusion, ...), kind=kOutput, calls=%fused_computation.86 | convolution fusion | flops 6456606720 | bytes 16807936 | tf_op jit(solution)/shard_map/dot_general | solution.py:89
  45.3 79.3 %while.28 = (s32[]{:T(128)}, f32[2,512,8,64]{1,0,3,2:T(2,128)}, f32[2,8,512]{2,1,0:T(8,128)S(1)}, s32[2]{0:T(128)S(1)}, s32[1024]{0:T(1024)S(1)}, /*index=5*/s32...) while((s32[]{:T(128)}, f32[2,512,8,64]{1,0,3,2:T(2,128)}, ...), condition=%wide.region_8.9_spmd.clone, body=%wide.region_5.8_spmd.clone.sunk | while | flops 1127216640 | bytes 64635104 | solution.py:112
  65.5 19.6 %dynamic_update_slice.19 = f32[2,512,8,64]{1,0,3,2:T(2,128)} dynamic-update-slice(f32[2,512,8,64]{1,0,3,2:T(2,128)} %get-tuple-element.475, f32[1,512,8,64]{1,0,3,2:T(1,128)} %copy.73, s32[]{:T(128)} %get-tuple-element.474, s32[]{:T(128)} %constant.40.clone.1..sunk, s32[]{:T(128)} %constant.40.clone.1..sunk, s32[]{:T(128)} %constant.40.clone.1..sunk) | dynamic-update-slice | bytes 2097156 | tf_op jit(solution)/shard_map/while/body/jit(dynamic_update_index_in_dim)/dynamic_update_slice | solution.py:112
  104.9 19.6 %dynamic_update_slice.19 = f32[2,512,8,64]{1,0,3,2:T(2,128)} dynamic-update-slice(f32[2,512,8,64]{1,0,3,2:T(2,128)} %get-tuple-element.475, f32[1,512,8,64]{1,0,3,2:T(1,128)} %copy.73, s32[]{:T(128)} %get-tuple-element.474, s32[]{:T(128)} %constant.40.clone.1..sunk, s32[]{:T(128)} %constant.40.clone.1..sunk, s32[]{:T(128)} %constant.40.clone.1..sunk) | dynamic-update-slice | bytes 2097156 | tf_op jit(solution)/shard_map/while/body/jit(dynamic_update_index_in_dim)/dynamic_update_slice | solution.py:112
  132.1 159.0 %while.29 = (s32[]{:T(128)}, f32[1024,8,64]{0,2,1:T(8,128)}, f32[1024,8,64]{0,2,1:T(8,128)}, f32[2,512,8,64]{1,0,3,2:T(2,128)}, s32[2]{0:T(128)S(1)}, /*index=5*...) while((s32[]{:T(128)}, f32[1024,8,64]{0,2,1:T(8,128)}, ...), condition=%wide.region_12.13_spmd.clone, body=%wide.region_10.12_spmd.clone.sunk | while | flops 2732324352 | bytes 187793712 | solution.py:166
  136.4 9.7 fusion.130
  146.1 13.8 %multiply_reduce_fusion.3 = (f32[8,512]{1,0:T(8,128)S(1)}, f32[8,512,1024]{2,1,0:T(8,128)}) fusion(f32[8,512,1024]{2,1,0:T(8,128)} %fusion.130, f32[8,512]{1,0:T(8,128)S(1)} %dynamic-slice_bitcast_fusion.2, bf16[1024,8,64]{0,2,1:T(8,128)(2,1)S(1)} %get-tuple-element.540, bf16[1024,8,64]{0,2,1:T(8,128)(2,1)S(1)} %copy-done.4, s32[]{:T(128)S(6)} %select_n.47, ...), kind=kOutput, calls=%fused_computation.23.clone.1 | convolution fusion | flops 562032640 | bytes 35684356 | tf_op jit(solution)/shard_map/while/body/eval_jaxpr/qhd,khd->hqk/dot_general | solution.py:55
  159.9 11.3 %multiply_convert_fusion.8 = bf16[8,512,1024]{2,1,0:T(8,128)(2,1)S(1)} fusion(f32[8,512,1024]{2,1,0:T(8,128)} %get-tuple-element.459, f32[8,512,1024]{2,1,0:T(8,128)} %fusion.130, f32[8,512]{1,0:T(8,128)S(1)} %get-tuple-element.460), kind=kLoop, calls=%fused_computation.22.clone.1 | loop fusion | flops 12582912 | bytes 41959424 | tf_op jit(solution)/shard_map/while/body/eval_jaxpr/convert_element_type | solution.py:153
  176.0 19.6 %dynamic_update_slice.20 = f32[2,512,8,64]{1,0,3,2:T(2,128)} dynamic-update-slice(f32[2,512,8,64]{1,0,3,2:T(2,128)} %get-tuple-element.519, f32[1,512,8,64]{1,0,3,2:T(1,128)} %copy.74, s32[]{:T(128)} %get-tuple-element.516, s32[]{:T(128)} %constant.40.clone.1..sunk.1, s32[]{:T(128)} %constant.40.clone.1..sunk.1, s32[]{:T(128)} %constant.40.clone.1..sunk.1) | dynamic-update-slice | bytes 2097156 | tf_op jit(solution)/shard_map/while/body/jit(dynamic_update_index_in_dim)/dynamic_update_slice | solution.py:112
  202.3 8.7 bitcast_add_fusion.6
  215.2 9.7 fusion.130
  224.8 13.7 %multiply_reduce_fusion.3 = (f32[8,512]{1,0:T(8,128)S(1)}, f32[8,512,1024]{2,1,0:T(8,128)}) fusion(f32[8,512,1024]{2,1,0:T(8,128)} %fusion.130, f32[8,512]{1,0:T(8,128)S(1)} %dynamic-slice_bitcast_fusion.2, bf16[1024,8,64]{0,2,1:T(8,128)(2,1)S(1)} %get-tuple-element.540, bf16[1024,8,64]{0,2,1:T(8,128)(2,1)S(1)} %copy-done.4, s32[]{:T(128)S(6)} %select_n.47, ...), kind=kOutput, calls=%fused_computation.23.clone.1 | convolution fusion | flops 562032640 | bytes 35684356 | tf_op jit(solution)/shard_map/while/body/eval_jaxpr/qhd,khd->hqk/dot_general | solution.py:55
  238.6 11.3 %multiply_convert_fusion.8 = bf16[8,512,1024]{2,1,0:T(8,128)(2,1)S(1)} fusion(f32[8,512,1024]{2,1,0:T(8,128)} %get-tuple-element.459, f32[8,512,1024]{2,1,0:T(8,128)} %fusion.130, f32[8,512]{1,0:T(8,128)S(1)} %get-tuple-element.460), kind=kLoop, calls=%fused_computation.22.clone.1 | loop fusion | flops 12582912 | bytes 41959424 | tf_op jit(solution)/shard_map/while/body/eval_jaxpr/convert_element_type | solution.py:153
  254.7 19.6 %dynamic_update_slice.20 = f32[2,512,8,64]{1,0,3,2:T(2,128)} dynamic-update-slice(f32[2,512,8,64]{1,0,3,2:T(2,128)} %get-tuple-element.519, f32[1,512,8,64]{1,0,3,2:T(1,128)} %copy.74, s32[]{:T(128)} %get-tuple-element.516, s32[]{:T(128)} %constant.40.clone.1..sunk.1, s32[]{:T(128)} %constant.40.clone.1..sunk.1, s32[]{:T(128)} %constant.40.clone.1..sunk.1) | dynamic-update-slice | bytes 2097156 | tf_op jit(solution)/shard_map/while/body/jit(dynamic_update_index_in_dim)/dynamic_update_slice | solution.py:112
  274.3 7.2 bitcast_add_fusion.5
  281.5 9.3 bitcast_add_fusion.6
  307.5 11.2 %copy.66 = bf16[256,8,2,1408]{3,1,2,0:T(8,128)(2,1)} copy(bf16[256,8,2,1408]{3,2,1,0:T(2,128)(2,1)} %bitcast.147) | data formatting | bytes 23068672
  318.8 15.2 %copy.41 = bf16[2816,2048]{1,0:T(8,128)(2,1)} copy(bf16[2816,2048]{0,1:T(8,128)(2,1)} %bitcast.143) | data formatting | bytes 23068672 | tf_op jit(solution)/shard_map/dot_general | solution.py:114
  334.0 19.1 %fusion.72 = f32[1024,2,1408]{2,0,1:T(8,128)} fusion(bf16[2,1408,2048]{2,1,0:T(8,128)(2,1)} %bitcast.148, bf16[1024,2048]{1,0:T(8,128)(2,1)} %param.15, f32[2048]{0:T(1024)S(1)} %copy-done.26, f32[2048]{0:T(1024)S(1)} %copy-done.22, f32[1024]{0:T(1024)S(1)} %copy-done.20, f32[1024]{0:T(1024)S(1)} %copy-done.18), kind=kOutput, calls=%fused_computation.130 | convolution fusion | flops 11823742976 | bytes 27287552 | tf_op jit(solution)/shard_map/dot_general | solution.py:114
  353.6 17.5 %fusion.59 = (bf16[1024,1,1408]{2,0,1:T(8,128)(2,1)}, bf16[1024,1,1408]{2,0,1:T(8,128)(2,1)}, bf16[1024,1408]{1,0:T(8,128)(2,1)}) fusion(f32[1024,2,1408]{2,0,1:T(8,128)} %fusion.72, bf16[1024,2048]{1,0:T(8,128)(2,1)} %param.25, bf16[1408,2048]{1,0:T(8,128)(2,1)} %param.24), kind=kOutput, calls=%fused_computation.88 | convolution fusion | flops 5927206912 | bytes 30146560 | tf_op jit(solution)/shard_map/to,fo->tf/dot_general | solution.py:136
  371.1 12.3 %fusion.76 = f32[1024,2048]{1,0:T(8,128)} fusion(bf16[1024,1408]{1,0:T(8,128)(2,1)} %get-tuple-element.292, bf16[1408,2048]{1,0:T(8,128)(2,1)} %param.24), kind=kOutput, calls=%fused_computation.132 | convolution fusion | flops 5905580032 | bytes 17039360 | tf_op jit(solution)/shard_map/dot_general | solution.py:125
  383.5 8.9 fusion.69
  392.4 20.2 %bitcast_add_fusion.2 = f32[1024,2048]{1,0:T(8,128)} fusion(f32[1024,2048,1]{1,0,2:T(8,128)} %fusion.69, bf16[2048,2,1408]{2,1,0:T(2,128)(2,1)} %param.23, bf16[1024,1,1408]{2,0,1:T(8,128)(2,1)} %get-tuple-element.291, bf16[1024,1,1408]{2,0,1:T(8,128)(2,1)} %get-tuple-element.290), kind=kOutput, calls=%fused_computation.69 | convolution fusion | flops 11816140800 | bytes 34078720 | tf_op jit(solution)/shard_map/tjf,djf->td/dot_general | solution.py:182
  412.7 9.1 convolution_add_fusion
  421.8 20.7 %fusion.57 = f32[2048,2,1408]{2,0,1:T(8,128)} fusion(bf16[1024,1,1408]{2,0,1:T(8,128)(2,1)} %get-tuple-element.291, bf16[1024,1,1408]{2,0,1:T(8,128)(2,1)} %get-tuple-element.290, bf16[1024,2048]{1,0:T(8,128)(2,1)} %param.15, f32[2048]{0:T(1024)S(1)} %copy-done.26, f32[2048]{0:T(1024)S(1)} %copy-done.22, f32[1024]{0:T(1024)S(1)} %copy-done.20, ...), kind=kOutput, calls=%fused_computation.84 | convolution fusion | flops 11835277312 | bytes 33054720 | tf_op jit(solution)/shard_map/td,tjf->djf/dot_general | solution.py:140
  442.6 7.1 fusion.63
  449.8 13.8 %fusion.77 = f32[1408,2048]{1,0:T(8,128)} fusion(bf16[1024,1408]{1,0:T(8,128)(2,1)} %get-tuple-element.292, bf16[1024,2048]{1,0:T(8,128)(2,1)} %param.25), kind=kOutput, calls=%fused_computation.133 | convolution fusion | flops 5905580032 | bytes 18612224 | tf_op jit(solution)/shard_map/tf,to->fo/dot_general | solution.py:131
  465.0 15.0 %fusion.68 = f32[2048,3,512]{2,0,1:T(8,128)} fusion(bf16[1024,1,512]{2,0,1:T(8,128)(2,1)} %copy.45, bf16[1024,1,512]{2,0,1:T(8,128)(2,1)} %copy.44, bf16[1024,1,512]{2,0,1:T(8,128)(2,1)S(1)} %copy-done.9, bf16[1024,2048]{1,0:T(8,128)(2,1)} %param.15, f32[2048]{0:T(1024)S(1)} %copy-done.26, f32[2048]{0:T(1024)S(1)} %copy-done.22, f32[1024]{0:T(1024)S(1)} %copy-done.20, ...), kind=kOutput, calls=%fused_computation.128 | convolution fusion | flops 6464471040 | bytes 19947520 | tf_op jit(solution)/shard_map/td,tjc->djc/dot_general | solution.py:172
  482.1 504.8 %all-reduce.4.cloned.1.call-done = (f32[1024,2048]{1,0:T(8,128)}, f32[1024,2048]{1,0:T(8,128)}) async-done(((f32[1024,2048]{1,0:T(8,128)}, f32[1024,2048]{1,0:T(8,128)}), (f32[1024,2048]{1,0:T(8,128)}, f32[1024,2048]{1,0:T(8,128)})) %all-reduce.4.cloned.1.call-update) | async-done | bytes 16777232 | tf_op jit(solution)/shard_map/psum | solution.py:128
  993.4 24.8 %all-reduce = (f32[2048]{0:T(1024)}, f32[2048]{0:T(1024)}, f32[3,512]{1,0:T(4,128)}) all-reduce(f32[2048]{0:T(1024)S(1)} %get-tuple-element.231, f32[2048]{0:T(1024)S(1)} %get-tuple-element.234, f32[3,512]{1,0:T(4,128)S(1)} %convert_reduce_fusion.1), channel_id=1, replica_groups=mesh['dp'=8,'mp'=4] {'dp'}, use_global_device_ids=true, to_apply=%region_17.18 | all-reduce | flops 5632 | bytes 45056 | tf_op jit(solution)/shard_map/psum | solution.py:193
  1018.2 13.6 %fusion.47 = (bf16[1024,2048]{1,0:T(8,128)(2,1)}, bf16[1024,2048]{1,0:T(8,128)(2,1)}) fusion(bf16[1024,2048]{1,0:T(8,128)(2,1)} %param.15, bf16[1024,2048]{1,0:T(8,128)(2,1)} %param.25, f32[1024,2048]{1,0:T(8,128)} %get-tuple-element.285, f32[1024]{0:T(1024)S(1)} %broadcast_multiply_fusion, f32[1024]{0:T(1024)S(1)} %broadcast_multiply_fusion.1, ...), kind=kLoop, calls=%fused_computation.65 | loop fusion | flops 27262976 | bytes 33579008 | tf_op jit(solution)/shard_map/convert_element_type | solution.py:192
  (160 shorter events, 113.3 us)
Async XLA Ops:
  8.0 116.5 %copy-start = (bf16[512,2048]{1,0:T(8,128)(2,1)S(1)}, bf16[512,2048]{1,0:T(8,128)(2,1)}, u32[]{:S(2)}) copy-start(bf16[512,2048]{1,0:T(8,128)(2,1)} %param.22) | copy-start | bytes 6291460
  8.0 978.9 %all-reduce.4.cloned.1.call-start = ((), (), s32[]{:S(2)}) async-start(), calls=%async_computation.8 | async-start | bytes 33554432 | tf_op jit(solution)/shard_map/psum | solution.py:128
  11.7 10.1 copy-start.17
  12.9 8.9 copy-start.19
  12.9 8.9 copy-start.21
  12.9 8.9 copy-start.24
  12.9 8.9 copy-start.25
  45.3 79.3 %copy-start.23 = (bf16[1024]{0:T(1024)(128)(2,1)S(1)}, bf16[1024]{0:T(1024)(128)(2,1)}, u32[]{:S(2)}) copy-start(bf16[1024]{0:T(1024)(128)(2,1)} %fusion.65) | copy-start | bytes 6148
  54.6 4.3 copy-start.2
  136.4 9.7 copy-start.4
  171.2 4.8 copy-start.1
  195.6 6.6 copy-start.5
  215.1 9.7 copy-start.4
  249.9 4.8 copy-start.1
  274.3 7.2 copy-start.5
  291.1 5.6 copy-start.14
  291.1 5.6 copy-start.16
  318.8 15.2 %copy-start.18 = (f32[1024]{0:T(1024)S(1)}, f32[1024]{0:T(1024)}, u32[]{:S(2)}) copy-start(f32[1024]{0:T(1024)} %copy-done.17) | copy-start | bytes 12292
  318.8 15.2 %copy-start.20 = (f32[1024]{0:T(1024)S(1)}, f32[1024]{0:T(1024)}, u32[]{:S(2)}) copy-start(f32[1024]{0:T(1024)} %copy-done.19) | copy-start | bytes 12292
  318.8 15.2 %copy-start.22 = (f32[2048]{0:T(1024)S(1)}, f32[2048]{0:T(1024)}, u32[]{:S(2)}) copy-start(f32[2048]{0:T(1024)} %param.18) | copy-start | bytes 24580
  318.8 15.2 %copy-start.26 = (f32[2048]{0:T(1024)S(1)}, f32[2048]{0:T(1024)}, u32[]{:S(2)}) copy-start(f32[2048]{0:T(1024)} %param.19) | copy-start | bytes 24580
  334.0 19.1 %copy-start.7 = (f32[2,512,8,64]{1,0,3,2:T(2,128)S(1)}, f32[2,512,8,64]{1,0,3,2:T(2,128)}, u32[]{:S(2)}) copy-start(f32[2,512,8,64]{1,0,3,2:T(2,128)} %get-tuple-element.131) | copy-start | bytes 6291460
  353.1 30.4 %slice-start = ((s8[6291456]{0:T(1024)(128)(4,1)}), s8[4194304]{0:T(1024)(128)(4,1)S(1)}, s32[]{:S(2)}) async-start(s8[6291456]{0:T(1024)(128)(4,1)} %bitcast.150), calls=%async_computation.9 | async-start | bytes 8388608
  353.5 59.2 %copy-start.6 = (f32[64,8,2,512]{3,1,2,0:T(8,128)}, f32[64,8,2,512]{3,1,2,0:T(8,128)S(1)}, u32[]{:S(2)}) copy-start(f32[64,8,2,512]{3,1,2,0:T(8,128)S(1)} %copy.65) | copy-start | bytes 6291460
  353.5 29.9 %slice-start.1 = ((s8[6291456]{0:T(1024)(128)(4,1)}), s8[2097152]{0:T(1024)(128)(4,1)S(1)}, s32[]{:S(2)}) async-start(s8[6291456]{0:T(1024)(128)(4,1)} %bitcast.150), calls=%async_computation.10 | async-start | bytes 4194304
  371.1 12.4 %copy-start.8 = (bf16[1024,1,512]{2,0,1:T(8,128)(2,1)S(1)}, bf16[1024,1,512]{2,0,1:T(8,128)(2,1)}, u32[]{:S(2)}) copy-start(bf16[1024,1,512]{2,0,1:T(8,128)(2,1)} %copy.43) | copy-start | bytes 3145732
  371.1 12.4 %copy-start.10 = (bf16[1024,1,512]{2,0,1:T(8,128)(2,1)S(1)}, bf16[1024,1,512]{2,0,1:T(8,128)(2,1)}, u32[]{:S(2)}) copy-start(bf16[1024,1,512]{2,0,1:T(8,128)(2,1)} %copy.44) | copy-start | bytes 3145732
  371.1 12.4 %copy-start.11 = (bf16[1024,1,512]{2,0,1:T(8,128)(2,1)S(1)}, bf16[1024,1,512]{2,0,1:T(8,128)(2,1)}, u32[]{:S(2)}) copy-start(bf16[1024,1,512]{2,0,1:T(8,128)(2,1)} %copy.45) | copy-start | bytes 3145732
  421.8 610.1 %reduce-scatter.9.cloned.1.call-start = ((), (), s32[]{:S(2)}) async-start(), calls=%async_computation.6 | async-start | bytes 25952256 | tf_op jit(solution)/shard_map/reduce_scatter | solution.py:177
  442.5 595.0 %reduce-scatter.7.cloned.1.call-start = ((), (), s32[]{:S(2)}) async-start(), calls=%async_computation.5 | async-start | bytes 4718592 | tf_op jit(solution)/shard_map/reduce_scatter | solution.py:176
  449.7 587.8 %reduce-scatter.11.cloned.1.call-start = ((), (), s32[]{:S(2)}) async-start(), calls=%async_computation.7 | async-start | bytes 12976128 | tf_op jit(solution)/shard_map/reduce_scatter | solution.py:178
  463.6 573.9 %reduce-scatter.5.cloned.1.call-start = ((), (), s32[]{:S(2)}) async-start(), calls=%async_computation.4 | async-start | bytes 14155776 | tf_op jit(solution)/shard_map/reduce_scatter | solution.py:175
  (6 other events, 15.6 us)
Sparse Core Ops, SparseCore 0:
  421.9 564.9 all-reduce.3
Sparse Core Ops, SparseCore 1:
  442.6 148.9 reduce-scatter.8
  595.3 50.9 reduce-scatter.6
  650.2 86.7 reduce-scatter.10
  741.0 91.8 reduce-scatter.4
where the time goes:
time: 1060 us; the launch traced here: 1050 us
  waiting for transfers between devices  505 us (48%)
  matrix products  262 us (25%)
  local copies, waits for them, and re-layouts  156 us (15%)
  other arithmetic  71.6 us (7%)
  blocking collectives  24.8 us (2%)
  between operations  17 us (2%)
    psum x1, waiting for transfers between devices, shards(): summed = lax.psum(partial_value, 'mp')  505 us
    dynamic_update_slice x8, local copies, waits for them, and re-layouts, shards(): attn_blocks, log_sums = lax.map(forward_block, starts)  86.9 us
    dot_general x4, matrix products, scores(): jnp.einsum('qhd,khd->hqk', part, key, preferred_element_type=jnp.float32)  36.8 us
    unnamed x54, local copies, waits for them, and re-layouts  28.3 us
    psum x1, blocking collectives, shards(): lax.psum((grad_bias, gain_product, shift_part), 'dp')  24.8 us
    convert_element_type x2, other arithmetic, backward_block(): d_score = d_score.astype(jnp.bfloat16)  22.7 us
  transfers between devices with their start and end apart: 5, of which 1 were waited for; matrix products, arithmetic and copies ran while one was open for 8% of the time, Pallas kernels for 0%

commit v1 on v0

--- a/solution.py
+++ b/solution.py
@@ -7,6 +7,20 @@
 ROT = 16
 DOCS = 4
 EPS = 1e-05
+
+
+def tails_lift(t0):
+    count_all = lax.axis_size("mp")
+    reply, v_next = (t0, 0)
+    while 1 << v_next < count_all:
+        block_next = lax.ppermute(
+            reply,
+            axis_name="mp",
+            perm=tuple(((hop_no, hop_no ^ 1 << v_next) for hop_no in range(count_all))),
+        )
+        reply = reply + block_next
+        v_next = v_next + 1
+    return reply
 
 
 def tables(seg, padding, count):
@@ -125,7 +139,7 @@
     partial_value = jnp.dot(attn, out_weight, preferred_element_type=jnp.float32) + jnp.dot(
         hidden, down_weight, preferred_element_type=jnp.float32
     )
-    summed = lax.psum(partial_value, "mp")
+    summed = tails_lift(partial_value)
     result = (xf + summed).astype(jnp.bfloat16)
     grad_out = jnp.einsum("ti,to->io", attn, y_grad, preferred_element_type=jnp.float32)
     grad_down = jnp.einsum("tf,to->fo", hidden, y_grad, preferred_element_type=jnp.float32)

time: 1060 us -> 1280 us (1.21)
  waiting for transfers between devices: 505 us -> 711 us
  other arithmetic: 71.6 us -> 87.6 us
    ppermute x0 -> x2, waiting for transfers between devices: none -> 711 us  [tails_lift(): lax.ppermute(reply, axis_name='mp', perm=tuple(((hop_no, hop_no ^ 1 << v_...]
    psum x1, waiting for transfers between devices: 505 us -> 0.02 us  [shards(): normalized_gradient = lax.psum(d_partial, 'mp')]
  transfers between devices with their start and end apart: 5 -> 7, of which waited for: 1 -> 2; matrix products, arithmetic and copies ran while one was open for 8% -> 9% of each run, Pallas kernels for 0% -> 0%
where the time goes in v1:
time: 1280 us; the launch traced here: 1270 us
  waiting for transfers between devices  711 us (56%)
  matrix products  253 us (20%)
  local copies, waits for them, and re-layouts  162 us (13%)
  other arithmetic  87.6 us (7%)
  blocking collectives  24.6 us (2%)
  between operations  16.9 us (1%)
    ppermute x2, waiting for transfers between devices, tails_lift(): lax.ppermute(reply, axis_name='mp', perm=tuple(((hop_no, hop_no ^ 1 << v_...  711 us
    dynamic_update_slice x8, local copies, waits for them, and re-layouts, shards(): attn_blocks, log_sums = lax.map(forward_block, starts)  86.9 us
    dot_general x4, matrix products, scores(): jnp.einsum('qhd,khd->hqk', part, key, preferred_element_type=jnp.float32)  36.8 us
    unnamed x54, local copies, waits for them, and re-layouts  33 us
  transfers between devices with their start and end apart: 7, of which 2 were waited for; matrix products, arithmetic and copies ran while one was open for 9% of the time, Pallas kernels for 0%

profile of v1, /device:TPU:0, one launch (start us, length us, event | category | flops | bytes accessed | tf_op | source)
XLA Modules:
  0.0 1269.4 jit_solution(2311608826617424284)
XLA Ops:
  12.9 8.9 copy.39
  21.8 10.5 broadcast_add_fusion
  45.3 78.9 %while.28 = (s32[]{:T(128)}, f32[2,512,8,64]{1,0,3,2:T(2,128)}, f32[2,8,512]{2,1,0:T(8,128)S(1)}, s32[2]{0:T(128)S(1)}, s32[1024]{0:T(1024)S(1)}, /*index=5*/s32...) while((s32[]{:T(128)}, f32[2,512,8,64]{1,0,3,2:T(2,128)}, ...), condition=%wide.region_8.9_spmd.clone, body=%wide.region_5.8_spmd.clone.sunk | while | flops 1127216640 | bytes 64635104 | solution.py:126
  65.2 19.6 %dynamic_update_slice.19 = f32[2,512,8,64]{1,0,3,2:T(2,128)} dynamic-update-slice(f32[2,512,8,64]{1,0,3,2:T(2,128)} %get-tuple-element.473, f32[1,512,8,64]{1,0,3,2:T(1,128)} %copy.73, s32[]{:T(128)} %get-tuple-element.472, s32[]{:T(128)} %constant.40.clone.1..sunk, s32[]{:T(128)} %constant.40.clone.1..sunk, s32[]{:T(128)} %constant.40.clone.1..sunk) | dynamic-update-slice | bytes 2097156 | tf_op jit(solution)/shard_map/while/body/jit(dynamic_update_index_in_dim)/dynamic_update_slice | solution.py:126
  104.6 19.6 %dynamic_update_slice.19 = f32[2,512,8,64]{1,0,3,2:T(2,128)} dynamic-update-slice(f32[2,512,8,64]{1,0,3,2:T(2,128)} %get-tuple-element.473, f32[1,512,8,64]{1,0,3,2:T(1,128)} %copy.73, s32[]{:T(128)} %get-tuple-element.472, s32[]{:T(128)} %constant.40.clone.1..sunk, s32[]{:T(128)} %constant.40.clone.1..sunk, s32[]{:T(128)} %constant.40.clone.1..sunk) | dynamic-update-slice | bytes 2097156 | tf_op jit(solution)/shard_map/while/body/jit(dynamic_update_index_in_dim)/dynamic_update_slice | solution.py:126
  131.7 159.2 %while.29 = (s32[]{:T(128)}, f32[1024,8,64]{0,2,1:T(8,128)}, f32[1024,8,64]{0,2,1:T(8,128)}, f32[2,512,8,64]{1,0,3,2:T(2,128)}, s32[2]{0:T(128)S(1)}, /*index=5*...) while((s32[]{:T(128)}, f32[1024,8,64]{0,2,1:T(8,128)}, ...), condition=%wide.region_11.12_spmd.clone, body=%wide.region_9.11_spmd.clone.sunk | while | flops 2732324352 | bytes 187793712 | solution.py:180
  136.1 9.7 fusion.130
  145.8 13.7 %multiply_reduce_fusion.3 = (f32[8,512]{1,0:T(8,128)S(1)}, f32[8,512,1024]{2,1,0:T(8,128)}) fusion(f32[8,512,1024]{2,1,0:T(8,128)} %fusion.130, f32[8,512]{1,0:T(8,128)S(1)} %dynamic-slice_bitcast_fusion.2, bf16[1024,8,64]{0,2,1:T(8,128)(2,1)S(1)} %get-tuple-element.538, bf16[1024,8,64]{0,2,1:T(8,128)(2,1)S(1)} %copy-done.5, s32[]{:T(128)S(6)} %select_n.47, ...), kind=kOutput, calls=%fused_computation.23.clone.1 | convolution fusion | flops 562032640 | bytes 35684356 | tf_op jit(solution)/shard_map/while/body/eval_jaxpr/qhd,khd->hqk/dot_general | solution.py:69
  159.5 11.3 multiply_convert_fusion.8
  175.7 19.6 %dynamic_update_slice.20 = f32[2,512,8,64]{1,0,3,2:T(2,128)} dynamic-update-slice(f32[2,512,8,64]{1,0,3,2:T(2,128)} %get-tuple-element.517, f32[1,512,8,64]{1,0,3,2:T(1,128)} %copy.74, s32[]{:T(128)} %get-tuple-element.514, s32[]{:T(128)} %constant.40.clone.1..sunk.1, s32[]{:T(128)} %constant.40.clone.1..sunk.1, s32[]{:T(128)} %constant.40.clone.1..sunk.1) | dynamic-update-slice | bytes 2097156 | tf_op jit(solution)/shard_map/while/body/jit(dynamic_update_index_in_dim)/dynamic_update_slice | solution.py:126
  202.0 8.7 bitcast_add_fusion.6
  214.8 9.7 fusion.130
  224.5 13.7 %multiply_reduce_fusion.3 = (f32[8,512]{1,0:T(8,128)S(1)}, f32[8,512,1024]{2,1,0:T(8,128)}) fusion(f32[8,512,1024]{2,1,0:T(8,128)} %fusion.130, f32[8,512]{1,0:T(8,128)S(1)} %dynamic-slice_bitcast_fusion.2, bf16[1024,8,64]{0,2,1:T(8,128)(2,1)S(1)} %get-tuple-element.538, bf16[1024,8,64]{0,2,1:T(8,128)(2,1)S(1)} %copy-done.5, s32[]{:T(128)S(6)} %select_n.47, ...), kind=kOutput, calls=%fused_computation.23.clone.1 | convolution fusion | flops 562032640 | bytes 35684356 | tf_op jit(solution)/shard_map/while/body/eval_jaxpr/qhd,khd->hqk/dot_general | solution.py:69
  238.2 11.3 multiply_convert_fusion.8
  254.4 19.6 %dynamic_update_slice.20 = f32[2,512,8,64]{1,0,3,2:T(2,128)} dynamic-update-slice(f32[2,512,8,64]{1,0,3,2:T(2,128)} %get-tuple-element.517, f32[1,512,8,64]{1,0,3,2:T(1,128)} %copy.74, s32[]{:T(128)} %get-tuple-element.514, s32[]{:T(128)} %constant.40.clone.1..sunk.1, s32[]{:T(128)} %constant.40.clone.1..sunk.1, s32[]{:T(128)} %constant.40.clone.1..sunk.1) | dynamic-update-slice | bytes 2097156 | tf_op jit(solution)/shard_map/while/body/jit(dynamic_update_index_in_dim)/dynamic_update_slice | solution.py:126
  274.0 7.2 bitcast_add_fusion.5
  281.2 9.3 bitcast_add_fusion.6
  312.4 11.2 copy.66
  323.6 15.2 %copy.41 = bf16[2816,2048]{1,0:T(8,128)(2,1)} copy(bf16[2816,2048]{0,1:T(8,128)(2,1)} %bitcast.143) | data formatting | bytes 23068672 | tf_op jit(solution)/shard_map/dot_general | solution.py:128
  338.8 19.1 %fusion.72 = f32[1024,2,1408]{2,0,1:T(8,128)} fusion(bf16[2,1408,2048]{2,1,0:T(8,128)(2,1)} %bitcast.148, bf16[1024,2048]{1,0:T(8,128)(2,1)} %param.15, f32[2048]{0:T(1024)S(1)} %copy-done.26, f32[2048]{0:T(1024)S(1)} %copy-done.22, f32[1024]{0:T(1024)S(1)} %copy-done.20, f32[1024]{0:T(1024)S(1)} %copy-done.18), kind=kOutput, calls=%fused_computation.130 | convolution fusion | flops 11823742976 | bytes 27287552 | tf_op jit(solution)/shard_map/dot_general | solution.py:128
  357.9 16.7 %fusion.59 = (bf16[1024,1,1408]{2,0,1:T(8,128)(2,1)}, bf16[1024,1,1408]{2,0,1:T(8,128)(2,1)}, bf16[1024,1408]{1,0:T(8,128)(2,1)}) fusion(f32[1024,2,1408]{2,0,1:T(8,128)} %fusion.72, bf16[1024,2048]{1,0:T(8,128)(2,1)} %param.25, bf16[1408,2048]{1,0:T(8,128)(2,1)} %param.24), kind=kOutput, calls=%fused_computation.88 | convolution fusion | flops 5927206912 | bytes 30146560 | tf_op jit(solution)/shard_map/to,fo->tf/dot_general | solution.py:150
  374.6 10.2 fusion.69
  384.8 20.2 %bitcast_add_fusion.2 = f32[1024,2048]{1,0:T(8,128)} fusion(f32[1024,2048,1]{1,0,2:T(8,128)} %fusion.69, bf16[2048,2,1408]{2,1,0:T(2,128)(2,1)} %param.23, bf16[1024,1,1408]{2,0,1:T(8,128)(2,1)} %get-tuple-element.289, bf16[1024,1,1408]{2,0,1:T(8,128)(2,1)} %get-tuple-element.288), kind=kOutput, calls=%fused_computation.69 | convolution fusion | flops 11816140800 | bytes 34078720 | tf_op jit(solution)/shard_map/tjf,djf->td/dot_general | solution.py:196
  405.0 20.9 %fusion.57 = f32[2048,2,1408]{2,0,1:T(8,128)} fusion(bf16[1024,1,1408]{2,0,1:T(8,128)(2,1)} %get-tuple-element.289, bf16[1024,1,1408]{2,0,1:T(8,128)(2,1)} %get-tuple-element.288, bf16[1024,2048]{1,0:T(8,128)(2,1)} %param.15, f32[2048]{0:T(1024)S(1)} %copy-done.26, f32[2048]{0:T(1024)S(1)} %copy-done.22, f32[1024]{0:T(1024)S(1)} %copy-done.20, ...), kind=kOutput, calls=%fused_computation.84 | convolution fusion | flops 11835277312 | bytes 33054720 | tf_op jit(solution)/shard_map/td,tjf->djf/dot_general | solution.py:154
  436.0 13.9 %fusion.77 = f32[1408,2048]{1,0:T(8,128)} fusion(bf16[1024,1408]{1,0:T(8,128)(2,1)} %get-tuple-element.290, bf16[1024,2048]{1,0:T(8,128)(2,1)} %param.25), kind=kOutput, calls=%fused_computation.133 | convolution fusion | flops 5905580032 | bytes 18612224 | tf_op jit(solution)/shard_map/tf,to->fo/dot_general | solution.py:145
  449.9 15.4 %fusion.68 = f32[2048,3,512]{2,0,1:T(8,128)} fusion(bf16[1024,1,512]{2,0,1:T(8,128)(2,1)} %copy.45, bf16[1024,1,512]{2,0,1:T(8,128)(2,1)} %copy.44, bf16[1024,1,512]{2,0,1:T(8,128)(2,1)S(1)} %copy.43, bf16[1024,2048]{1,0:T(8,128)(2,1)} %param.15, f32[2048]{0:T(1024)S(1)} %copy-done.26, f32[2048]{0:T(1024)S(1)} %copy-done.22, f32[1024]{0:T(1024)S(1)} %copy-done.20, ...), kind=kOutput, calls=%fused_computation.128 | convolution fusion | flops 6464471040 | bytes 19947520 | tf_op jit(solution)/shard_map/td,tjc->djc/dot_general | solution.py:186
  465.4 9.7 fusion.76
  484.5 380.3 %collective-permute-done = f32[1024,2048]{1,0:T(8,128)} collective-permute-done((f32[1024,2048]{1,0:T(8,128)S(1)}, f32[1024,2048]{1,0:T(8,128)}, u32[]{:S(2)}, u32[]{:S(2)}) %collective-permute-start) | collective-permute-done | bytes 8388640 | tf_op jit(solution)/shard_map/ppermute | solution.py:16
  864.7 11.8 add.145
  884.1 24.6 %all-reduce = (f32[2048]{0:T(1024)}, f32[2048]{0:T(1024)}, f32[3,512]{1,0:T(4,128)}) all-reduce(f32[2048]{0:T(1024)S(1)} %get-tuple-element.231, f32[2048]{0:T(1024)S(1)} %get-tuple-element.234, f32[3,512]{1,0:T(4,128)S(1)} %convert_reduce_fusion.1), channel_id=1, replica_groups=mesh['dp'=8,'mp'=4] {'dp'}, use_global_device_ids=true, to_apply=%region_16.17 | all-reduce | flops 5632 | bytes 45056 | tf_op jit(solution)/shard_map/psum | solution.py:207
  908.7 331.0 %collective-permute-done.1 = f32[1024,2048]{1,0:T(8,128)} collective-permute-done((f32[1024,2048]{1,0:T(8,128)}, f32[1024,2048]{1,0:T(8,128)}, u32[]{:S(2)}, u32[]{:S(2)}) %collective-permute-start.1) | collective-permute-done | bytes 8388640 | tf_op jit(solution)/shard_map/ppermute | solution.py:16
  1239.7 16.2 %fusion.47 = (bf16[1024,2048]{1,0:T(8,128)(2,1)}, bf16[1024,2048]{1,0:T(8,128)(2,1)}) fusion(bf16[1024,2048]{1,0:T(8,128)(2,1)} %param.15, bf16[1024,2048]{1,0:T(8,128)(2,1)} %param.25, f32[1024,2048]{1,0:T(8,128)} %all-reduce.3.cloned.1.call-done, f32[1024]{0:T(1024)S(1)} %broadcast_multiply_fusion, f32[1024]{0:T(1024)S(1)} %broadcast_multiply_fusion.1, ...), kind=kLoop, calls=%fused_computation.65 | loop fusion | flops 29360128 | bytes 41967616 | tf_op jit(solution)/shard_map/convert_element_type | solution.py:206
  (165 shorter events, 134.8 us)
Async XLA Ops:
  8.0 116.2 %copy-start = (bf16[512,2048]{1,0:T(8,128)(2,1)S(1)}, bf16[512,2048]{1,0:T(8,128)(2,1)}, u32[]{:S(2)}) copy-start(bf16[512,2048]{1,0:T(8,128)(2,1)} %param.22) | copy-start | bytes 6291460
  8.0 869.3 %all-reduce.3.cloned.1.call-start = ((), (), s32[]{:S(2)}) async-start(), calls=%async_computation.4 | async-start | bytes 16777216 | tf_op jit(solution)/shard_map/psum | solution.py:197
  11.7 10.1 copy-start.17
  12.9 8.9 copy-start.19
  12.9 8.9 copy-start.21
  12.9 8.9 copy-start.24
  12.9 8.9 copy-start.25
  45.3 78.9 %copy-start.23 = (bf16[1024]{0:T(1024)(128)(2,1)S(1)}, bf16[1024]{0:T(1024)(128)(2,1)}, u32[]{:S(2)}) copy-start(bf16[1024]{0:T(1024)(128)(2,1)} %fusion.65) | copy-start | bytes 6148
  136.1 9.7 copy-start.5
  170.9 4.8 copy-start.1
  195.3 6.6 copy-start.6
  214.8 9.7 copy-start.5
  249.6 4.8 copy-start.1
  274.0 7.2 copy-start.6
  290.9 5.6 copy-start.14
  290.9 5.6 copy-start.16
  323.6 15.2 %copy-start.18 = (f32[1024]{0:T(1024)S(1)}, f32[1024]{0:T(1024)}, u32[]{:S(2)}) copy-start(f32[1024]{0:T(1024)} %copy-done.17) | copy-start | bytes 12292
  323.6 15.2 %copy-start.20 = (f32[1024]{0:T(1024)S(1)}, f32[1024]{0:T(1024)}, u32[]{:S(2)}) copy-start(f32[1024]{0:T(1024)} %copy-done.19) | copy-start | bytes 12292
  323.6 15.2 %copy-start.22 = (f32[2048]{0:T(1024)S(1)}, f32[2048]{0:T(1024)}, u32[]{:S(2)}) copy-start(f32[2048]{0:T(1024)} %param.18) | copy-start | bytes 24580
  323.6 15.2 %copy-start.26 = (f32[2048]{0:T(1024)S(1)}, f32[2048]{0:T(1024)}, u32[]{:S(2)}) copy-start(f32[2048]{0:T(1024)} %param.19) | copy-start | bytes 24580
  338.8 35.8 %slice-start = ((s8[6291456]{0:T(1024)(128)(4,1)}), s8[4194304]{0:T(1024)(128)(4,1)S(1)}, s32[]{:S(2)}) async-start(s8[6291456]{0:T(1024)(128)(4,1)} %bitcast.150), calls=%async_computation.9 | async-start | bytes 8388608
  357.9 16.7 %slice-start.1 = ((s8[6291456]{0:T(1024)(128)(4,1)}), s8[2097152]{0:T(1024)(128)(4,1)S(1)}, s32[]{:S(2)}) async-start(s8[6291456]{0:T(1024)(128)(4,1)} %bitcast.150), calls=%async_computation.10 | async-start | bytes 4194304
  357.9 16.7 %copy-start.9 = (bf16[1024,1,512]{2,0,1:T(8,128)(2,1)S(1)}, bf16[1024,1,512]{2,0,1:T(8,128)(2,1)}, u32[]{:S(2)}) copy-start(bf16[1024,1,512]{2,0,1:T(8,128)(2,1)} %copy.44) | copy-start | bytes 3145732
  405.0 851.0 %reduce-scatter.9.cloned.1.call-start = ((), (), s32[]{:S(2)}) async-start(), calls=%async_computation.7 | async-start | bytes 25952256 | tf_op jit(solution)/shard_map/reduce_scatter | solution.py:191
  425.9 835.6 %reduce-scatter.7.cloned.1.call-start = ((), (), s32[]{:S(2)}) async-start(), calls=%async_computation.6 | async-start | bytes 4718592 | tf_op jit(solution)/shard_map/reduce_scatter | solution.py:190
  435.9 825.6 %reduce-scatter.11.cloned.1.call-start = ((), (), s32[]{:S(2)}) async-start(), calls=%async_computation.8 | async-start | bytes 12976128 | tf_op jit(solution)/shard_map/reduce_scatter | solution.py:192
  449.9 811.7 %reduce-scatter.5.cloned.1.call-start = ((), (), s32[]{:S(2)}) async-start(), calls=%async_computation.5 | async-start | bytes 14155776 | tf_op jit(solution)/shard_map/reduce_scatter | solution.py:189
  465.3 9.7 copy-start.8
  480.8 396.1 %copy-start.10 = (bf16[1024,1,512]{2,0,1:T(8,128)(2,1)S(1)}, bf16[1024,1,512]{2,0,1:T(8,128)(2,1)}, u32[]{:S(2)}) copy-start(bf16[1024,1,512]{2,0,1:T(8,128)(2,1)} %copy.44) | copy-start | bytes 3145732
  480.8 396.1 %copy-start.11 = (bf16[1024,1,512]{2,0,1:T(8,128)(2,1)S(1)}, bf16[1024,1,512]{2,0,1:T(8,128)(2,1)}, u32[]{:S(2)}) copy-start(bf16[1024,1,512]{2,0,1:T(8,128)(2,1)} %copy.45) | copy-start | bytes 3145732
  480.8 383.9 %collective-permute-start = (f32[1024,2048]{1,0:T(8,128)S(1)}, f32[1024,2048]{1,0:T(8,128)}, u32[]{:S(2)}, u32[]{:S(2)}) collective-permute-start(f32[1024,2048]{1,0:T(8,128)S(1)} %convolution_add_fusion), channel_id=1, source_target_pairs={{0,1},{1,0},{2,3},{3,2},{4,5},{5,4},{6,7},{7,6},{8,9},{9,8},{10,11... | collective-permute-start | bytes 25165832 | tf_op jit(solution)/shard_map/ppermute | solution.py:16
  876.5 363.2 %collective-permute-start.1 = (f32[1024,2048]{1,0:T(8,128)}, f32[1024,2048]{1,0:T(8,128)}, u32[]{:S(2)}, u32[]{:S(2)}) collective-permute-start(f32[1024,2048]{1,0:T(8,128)} %add.145), channel_id=1, source_target_pairs={{0,2},{1,3},{2,0},{3,1},{4,6},{5,7},{6,4},{7,5},{8,10},{9,11},{10,... | collective-permute-start | bytes 25165832 | tf_op jit(solution)/shard_map/ppermute | solution.py:16
  (8 other events, 23.0 us)
Sparse Core Ops, SparseCore 0:
  405.1 458.0 all-reduce.2
Sparse Core Ops, SparseCore 1:
  426.0 148.9 reduce-scatter.8
  578.8 50.9 reduce-scatter.6
  633.6 86.7 reduce-scatter.10
  724.4 91.9 reduce-scatter.4
